TPU v7x, 128 devices: a whole 4x4x4 slice. The times are simulated.
128 devices in a mesh: seq: 128 (over x, y, z, core).
Axes of the slice: x: 4, y: 4, z: 4, core: 2. Of those that a mesh axis runs over, the one named last changes fastest.
Arguments:
- inputs: bfloat16 [131072, 768], P('seq'), may hold values from -6 to 6
- weight_one: bfloat16 [768, 3, 768], P('seq'), may hold values from -0.125 to 0.125
- weight_two: bfloat16 [768, 3, 768], P('seq'), may hold values from -0.125 to 0.125
- cotangent: bfloat16 [131072, 768], P('seq'), may hold values from -6 to 6
Outputs:
- outputs: bfloat16 [131072, 768], P('seq')
- input_grad: bfloat16 [131072, 768], P('seq')
- grad_one: float32 [768, 3, 768], P('seq')
- grad_two: float32 [768, 3, 768], P('seq')
All inputs are finite; a program needn't handle non-finite values.
Results may differ from a plain program's by a relative error of at most 0.0056.
Values may be sent and summed in bfloat16 or wider, within the bound.
A program may use at most 128 MiB of HBM per device.

v0:
```python
import math
import jax
import jax.numpy as jnp
from jax import lax
from jax.sharding import PartitionSpec as P

DILATION_A = 32
DILATION_B = 64


def padded_2(block, sides, width):
    for axis, dim in sides:
        count = lax.axis_size(axis)
        forward = [(i, i + 1) for i in range(count - 1)]
        backward = [(target, source) for source, target in forward]
        low = lax.ppermute(
            lax.slice_in_dim(block, block.shape[dim] - width, None, axis=dim), axis, forward
        )
        high = lax.ppermute(lax.slice_in_dim(block, 0, width, axis=dim), axis, backward)
        block = jnp.concatenate([low, block, high], axis=dim)
    return block


def normalize(layer_in):
    residual_in = layer_in.astype(jnp.float32)
    inv_rms = lax.rsqrt(jnp.mean(residual_in * residual_in, axis=-1, keepdims=True) + 1e-06)
    normed = residual_in * inv_rms
    active = (0.5 * normed * (1.0 + jax.scipy.special.erf(normed * 0.7071067811865476))).astype(
        jnp.bfloat16
    )
    return (residual_in, normed, inv_rms, active)


def slope_of(normed):
    return (
        0.5 * (1.0 + jax.scipy.special.erf(normed * 0.7071067811865476))
        + normed * jnp.exp(-0.5 * normed * normed) * 0.3989422804014327
    )


def fetch_forward(shard):
    return lax.all_gather(shard, "seq", axis=0, tiled=True)


def fetch_backward(shard):
    return lax.all_gather(shard, "seq", axis=0, tiled=True)


def forward_layer(layer_in, weight, spacing):
    residual_in, normed, inv_rms, active = normalize(layer_in)
    padded = padded_2(active, (("seq", 0),), spacing)
    length = layer_in.shape[0]
    mixed = jnp.zeros((length, weight.shape[2]), jnp.float32)
    for tap in range(3):
        mixed = mixed + jnp.dot(
            padded[tap * spacing : tap * spacing + length],
            weight[:, tap, :],
            preferred_element_type=jnp.float32,
        )
    return ((residual_in + mixed).astype(jnp.bfloat16), padded, normed, inv_rms)


def weight_term(padded, grad_out, spacing, grad_scale):
    length = grad_out.shape[0]
    terms = []
    for tap in range(3):
        window = padded[tap * spacing : tap * spacing + length]
        terms.append(
            lax.dot_general(
                window, grad_out, (((0,), (0,)), ((), ())), preferred_element_type=jnp.float32
            )
        )
    return jnp.stack(terms, axis=1) * grad_scale


def reduce_layer(padded, grad_out, spacing, grad_scale):
    whole_term = weight_term(padded, grad_out, spacing, grad_scale)
    return lax.psum_scatter(whole_term, "seq", scatter_dimension=0, tiled=True)


def backward_layer(grad_out, normed, inv_rms, weight, spacing):
    length = grad_out.shape[0]
    grad_pad = padded_2(grad_out, (("seq", 0),), spacing)
    act_grad = jnp.zeros((length, weight.shape[0]), jnp.float32)
    for tap in range(3):
        start_row = (2 - tap) * spacing
        act_grad = act_grad + lax.dot_general(
            grad_pad[start_row : start_row + length],
            weight[:, tap, :],
            (((1,), (1,)), ((), ())),
            preferred_element_type=jnp.float32,
        )
    norm_grad = act_grad * slope_of(normed)
    passed = grad_out.astype(jnp.float32) + inv_rms * (
        norm_grad - normed * jnp.mean(norm_grad * normed, axis=-1, keepdims=True)
    )
    return passed.astype(jnp.bfloat16)


def per_device(inputs, weight_one, weight_two, cotangent):
    grad_scale = 1.0 / math.sqrt(inputs.shape[0] * lax.axis_size("seq"))
    full_one = fetch_forward(weight_one)
    hidden, pad_one, normed_one, inv_one = forward_layer(inputs, full_one, DILATION_A)
    full_two = fetch_forward(weight_two)
    outputs, pad_two, normed_two, inv_two = forward_layer(hidden, full_two, DILATION_B)
    back_two = fetch_backward(weight_two)
    hidden_grad = backward_layer(cotangent, normed_two, inv_two, back_two, DILATION_B)
    grad_two = reduce_layer(pad_two, cotangent, DILATION_B, grad_scale)
    back_one = fetch_backward(weight_one)
    input_grad = backward_layer(hidden_grad, normed_one, inv_one, back_one, DILATION_A)
    grad_one = reduce_layer(pad_one, hidden_grad, DILATION_A, grad_scale)
    return (outputs, input_grad, grad_one, grad_two)


def solution(mesh):
    in_specs = (P("seq", None), P("seq", None, None), P("seq", None, None), P("seq", None))
    out_specs = (P("seq", None), P("seq", None), P("seq", None, None), P("seq", None, None))
    return jax.shard_map(
        per_device, mesh=mesh, in_specs=in_specs, out_specs=out_specs, check_vma=False
    )
```

profile of v0, /device:TPU:1, one launch (start us, length us, event | category | flops | bytes accessed | tf_op | source)
XLA Modules:
  0.0 380.1 jit_solution(17278720018428972216)
XLA Ops:
  8.7 1.9 fusion.22
  13.0 3.3 collective-permute-start.1
  16.4 3.5 collective-permute-start
  19.9 2.4 collective-permute-start.5
  22.3 1.9 collective-permute-start.4
  24.3 57.8 %all-gather.3.cloned.1.call-done = bf16[768,3,768]{2,1,0:T(4,128)(2,1)} async-done(((bf16[6,3,768]{2,1,0:T(4,128)(2,1)}), bf16[768,3,768]{2,1,0:T(4,128)(2,1)}) %all-gather.3.cloned.1.call-update) | async-done | bytes 3538960 | tf_op jit(solution)/shard_map/all_gather | solution.py:42
  82.0 12.4 %fusion.69 = (bf16[768,1,768]{2,1,0:T(2,128)(2,1)}, bf16[768,1,768]{2,1,0:T(2,128)(2,1)S(1)}, bf16[768,1,768]{2,1,0:T(2,128)(2,1)}) fusion(bf16[768,3,768]{2,1,0:T(4,128)(2,1)} %all-gather.3.cloned.1.call-done), kind=kLoop, calls=%fused_computation.105 | loop fusion | bytes 7077888 | tf_op jit(solution)/shard_map/slice | solution.py:57
  95.8 3.1 fusion.53
  98.9 50.7 %all-gather.5.cloned.1.call-done = bf16[768,3,768]{2,1,0:T(4,128)(2,1)} async-done(((bf16[6,3,768]{2,1,0:T(4,128)(2,1)}), bf16[768,3,768]{2,1,0:T(4,128)(2,1)}) %all-gather.5.cloned.1.call-update) | async-done | bytes 3538960 | tf_op jit(solution)/shard_map/all_gather | solution.py:42
  149.6 11.4 %fusion.68 = (bf16[768,1,768]{2,1,0:T(2,128)(2,1)S(1)}, bf16[768,1,768]{2,1,0:T(2,128)(2,1)S(1)}, bf16[768,1,768]{2,1,0:T(2,128)(2,1)S(1)}) fusion(bf16[768,3,768]{2,1,0:T(4,128)(2,1)} %all-gather.5.cloned.1.call-done), kind=kLoop, calls=%fused_computation.104 | loop fusion | bytes 7077888 | tf_op jit(solution)/shard_map/slice | solution.py:57
  162.5 1.9 copy-done.11
  165.6 2.2 fusion.48
  167.8 2.5 fusion.46
  170.5 2.6 fusion.36
  173.1 2.6 fusion.35
  175.8 2.1 fusion.31
  179.4 1.9 collective-permute-start.2
  181.4 2.4 collective-permute-start.3
  183.8 1.5 convolution_bitcast_fusion.4
  185.3 2.3 convolution_bitcast_fusion.3
  187.5 2.3 convolution_bitcast_fusion.5
  189.8 3.3 maximum_multiply_fusion
  193.1 1.5 convolution_bitcast_fusion
  194.6 1.5 convolution_bitcast_fusion.2
  196.1 3.2 maximum_multiply_fusion.1
  200.2 2.2 collective-permute-start.6
  202.4 3.1 fusion.55
  206.9 4.1 %collective-permute-start.7 = (bf16[32,768]{1,0:T(8,128)(2,1)S(1)}, bf16[32,768]{1,0:T(8,128)(2,1)S(1)}, u32[]{:S(2)}, u32[]{:S(2)}) collective-permute-start(bf16[32,768]{1,0:T(8,128)(2,1)S(1)} %get-tuple-element.26), channel_id=1, source_target_pairs={{0,1},{1,2},{2,3},{3,4},{4,5},{5,6},{6,7},{7,8},{8,9},{9,10},{10,1... | collective-permute-start | bytes 147464 | tf_op jit(solution)/shard_map/ppermute | solution.py:16
  212.5 2.6 fusion.21
  215.2 2.0 fusion.17
  219.5 2.8 fusion.37
  222.3 148.9 %all-reduce.5.cloned.1.call-done = (f32[768,3,768]{2,0,1:T(8,128)}, f32[768,3,768]{2,0,1:T(8,128)}) async-done(((f32[768,3,768]{2,0,1:T(8,128)}, f32[768,3,768]{2,0,1:T(8,128)}), (f32[768,3,768]{2,0,1:T(8,128)}, f32[768,3,768]{2,0,1:T(8,128)})) %all-reduce.5.cloned.1.call-update) | async-done | bytes 14155792
  (74 shorter events, 17.9 us)
Async XLA Ops:
  7.2 3.5 copy-start
  7.2 74.8 %all-gather.3.cloned.1.call-start = ((), (), s32[]{:S(2)}) async-start(), calls=%async_computation | async-start | bytes 4755456 | tf_op jit(solution)/shard_map/all_gather | solution.py:42
  7.9 141.7 %all-gather.5.cloned.1.call-start = ((), (), s32[]{:S(2)}) async-start(), calls=%async_computation.1 | async-start | bytes 4755456 | tf_op jit(solution)/shard_map/all_gather | solution.py:42
  8.7 11.2 %copy-start.16 = (bf16[1024,768]{1,0:T(8,128)(2,1)S(1)}, bf16[1024,768]{1,0:T(8,128)(2,1)}, u32[]{:S(2)}) copy-start(bf16[1024,768]{1,0:T(8,128)(2,1)} %param.7) | copy-start | bytes 4718596
  8.7 362.6 %all-reduce.5.cloned.1.call-start = ((), (), s32[]{:S(2)}) async-start(), calls=%async_computation.2 | async-start | bytes 28311552
  13.0 157.3 %collective-permute-start.1 = (bf16[32,768]{1,0:T(8,128)(2,1)S(1)}, bf16[32,768]{1,0:T(8,128)(2,1)}, u32[]{:S(2)}, u32[]{:S(2)}) collective-permute-start(bf16[32,768]{1,0:T(8,128)(2,1)S(1)} %get-tuple-element.32), channel_id=1, source_target_pairs={{1,0},{2,1},{3,2},{4,3},{5,4},{6,5},{7,6},{8,7},{9,8},{10,9},{11,1... | collective-permute-start | bytes 147464 | tf_op jit(solution)/shard_map/ppermute | solution.py:19
  16.4 146.1 %collective-permute-start = (bf16[32,768]{1,0:T(8,128)(2,1)S(1)}, bf16[32,768]{1,0:T(8,128)(2,1)}, u32[]{:S(2)}, u32[]{:S(2)}) collective-permute-start(bf16[32,768]{1,0:T(8,128)(2,1)S(1)} %get-tuple-element.33), channel_id=1, source_target_pairs={{0,1},{1,2},{2,3},{3,4},{4,5},{5,6},{6,7},{7,8},{8,9},{9,10},{10,1... | collective-permute-start | bytes 147464 | tf_op jit(solution)/shard_map/ppermute | solution.py:16
  19.9 153.2 %collective-permute-start.5 = (bf16[64,768]{1,0:T(8,128)(2,1)S(1)}, bf16[64,768]{1,0:T(8,128)(2,1)S(1)}, u32[]{:S(2)}, u32[]{:S(2)}) collective-permute-start(bf16[64,768]{1,0:T(8,128)(2,1)S(1)} %get-tuple-element.28), channel_id=1, source_target_pairs={{0,1},{1,2},{2,3},{3,4},{4,5},{5,6},{6,7},{7,8},{8,9},{9,10},{10,1... | collective-permute-start | bytes 294920 | tf_op jit(solution)/shard_map/ppermute | solution.py:16
  22.3 145.5 %collective-permute-start.4 = (bf16[64,768]{1,0:T(8,128)(2,1)S(1)}, bf16[64,768]{1,0:T(8,128)(2,1)}, u32[]{:S(2)}, u32[]{:S(2)}) collective-permute-start(bf16[64,768]{1,0:T(8,128)(2,1)S(1)} %get-tuple-element.29), channel_id=1, source_target_pairs={{1,0},{2,1},{3,2},{4,3},{5,4},{6,5},{7,6},{8,7},{9,8},{10,9},{11,1... | collective-permute-start | bytes 294920 | tf_op jit(solution)/shard_map/ppermute | solution.py:19
  82.0 13.8 %copy-start.19 = (bf16[1024,768]{1,0:T(8,128)(2,1)S(1)}, bf16[1024,768]{1,0:T(8,128)(2,1)}, u32[]{:S(2)}) copy-start(bf16[1024,768]{1,0:T(8,128)(2,1)} %copy-done.18) | copy-start | bytes 4718596
  94.4 1.4 copy-start.13
  161.0 1.5 copy-start.15
  161.0 6.8 %copy-start.7 = (bf16[768,1,768]{2,1,0:T(2,128)(2,1)}, bf16[768,1,768]{2,1,0:T(2,128)(2,1)S(1)}, u32[]{:S(2)}) copy-start(bf16[768,1,768]{2,1,0:T(2,128)(2,1)S(1)} %get-tuple-element.20) | copy-start | bytes 3538948
  161.0 12.1 %copy-start.5 = (bf16[768,1,768]{2,1,0:T(2,128)(2,1)}, bf16[768,1,768]{2,1,0:T(2,128)(2,1)S(1)}, u32[]{:S(2)}) copy-start(bf16[768,1,768]{2,1,0:T(2,128)(2,1)S(1)} %get-tuple-element.18) | copy-start | bytes 3538948
  161.0 3.4 copy-start.11
  161.0 4.6 %copy-start.20 = (bf16[1024,768]{1,0:T(8,128)(2,1)S(1)}, bf16[1024,768]{1,0:T(8,128)(2,1)}, u32[]{:S(2)}) copy-start(bf16[1024,768]{1,0:T(8,128)(2,1)} %copy-done.18) | copy-start | bytes 4718596
  167.8 2.5 copy-start.9
  167.8 2.6 copy-start.21
  173.1 2.7 copy-start.3
  173.1 2.7 copy-start.17
  177.9 9.6 %copy-start.1 = (bf16[1024,768]{1,0:T(8,128)(2,1)}, bf16[1024,768]{1,0:T(8,128)(2,1)S(1)}, u32[]{:S(2)}) copy-start(bf16[1024,768]{1,0:T(8,128)(2,1)S(1)} %get-tuple-element.24) | copy-start | bytes 4718596
  179.4 15.1 %collective-permute-start.2 = (bf16[64,768]{1,0:T(8,128)(2,1)S(1)}, bf16[64,768]{1,0:T(8,128)(2,1)S(1)}, u32[]{:S(2)}, u32[]{:S(2)}) collective-permute-start(bf16[64,768]{1,0:T(8,128)(2,1)S(1)} %get-tuple-element.31), channel_id=1, source_target_pairs={{0,1},{1,2},{2,3},{3,4},{4,5},{5,6},{6,7},{7,8},{8,9},{9,10},{10,1... | collective-permute-start | bytes 294920 | tf_op jit(solution)/shard_map/ppermute | solution.py:16
  181.4 11.7 %collective-permute-start.3 = (bf16[64,768]{1,0:T(8,128)(2,1)S(1)}, bf16[64,768]{1,0:T(8,128)(2,1)S(1)}, u32[]{:S(2)}, u32[]{:S(2)}) collective-permute-start(bf16[64,768]{1,0:T(8,128)(2,1)S(1)} %get-tuple-element.30), channel_id=1, source_target_pairs={{1,0},{2,1},{3,2},{4,3},{5,4},{6,5},{7,6},{8,7},{9,8},{10,9},{11,1... | collective-permute-start | bytes 294920 | tf_op jit(solution)/shard_map/ppermute | solution.py:19
  200.2 5.3 %copy-start.2 = (bf16[1024,768]{1,0:T(8,128)(2,1)S(1)}, bf16[1024,768]{1,0:T(8,128)(2,1)}, u32[]{:S(2)}) copy-start(bf16[1024,768]{1,0:T(8,128)(2,1)} %copy-done.1) | copy-start | bytes 4718596
  200.2 5.3 %copy-start.14 = (bf16[768,1,768]{2,1,0:T(2,128)(2,1)S(1)}, bf16[768,1,768]{2,1,0:T(2,128)(2,1)}, u32[]{:S(2)}) copy-start(bf16[768,1,768]{2,1,0:T(2,128)(2,1)} %copy-done.13) | copy-start | bytes 3538948
  200.2 10.9 %collective-permute-start.6 = (bf16[32,768]{1,0:T(8,128)(2,1)S(1)}, bf16[32,768]{1,0:T(8,128)(2,1)S(1)}, u32[]{:S(2)}, u32[]{:S(2)}) collective-permute-start(bf16[32,768]{1,0:T(8,128)(2,1)S(1)} %get-tuple-element.27), channel_id=1, source_target_pairs={{1,0},{2,1},{3,2},{4,3},{5,4},{6,5},{7,6},{8,7},{9,8},{10,9},{11,1... | collective-permute-start | bytes 147464 | tf_op jit(solution)/shard_map/ppermute | solution.py:19
  205.4 5.6 %copy-start.12 = (bf16[768,1,768]{2,1,0:T(2,128)(2,1)S(1)}, bf16[768,1,768]{2,1,0:T(2,128)(2,1)}, u32[]{:S(2)}) copy-start(bf16[768,1,768]{2,1,0:T(2,128)(2,1)} %get-tuple-element.23) | copy-start | bytes 3538948
  206.9 5.6 %copy-start.10 = (bf16[768,1,768]{2,1,0:T(2,128)(2,1)S(1)}, bf16[768,1,768]{2,1,0:T(2,128)(2,1)}, u32[]{:S(2)}) copy-start(bf16[768,1,768]{2,1,0:T(2,128)(2,1)} %get-tuple-element.21) | copy-start | bytes 3538948
  206.9 5.6 %collective-permute-start.7 = (bf16[32,768]{1,0:T(8,128)(2,1)S(1)}, bf16[32,768]{1,0:T(8,128)(2,1)S(1)}, u32[]{:S(2)}, u32[]{:S(2)}) collective-permute-start(bf16[32,768]{1,0:T(8,128)(2,1)S(1)} %get-tuple-element.26), channel_id=1, source_target_pairs={{0,1},{1,2},{2,3},{3,4},{4,5},{5,6},{6,7},{7,8},{8,9},{9,10},{10,1... | collective-permute-start | bytes 147464 | tf_op jit(solution)/shard_map/ppermute | solution.py:16
  215.2 2.0 copy-start.8
  217.2 1.5 copy-start.4
  217.2 2.3 copy-start.6
  (1 other events, 1.1 us)
Sparse Core Ops, SparseCore 0:
  11.0 70.9 all-gather.2
  85.0 64.5 all-gather.4
  199.4 171.7 all-reduce.4
where the time goes:
time: 381 us; the launch traced here: 380 us
  waiting for transfers between devices  259 us (68%)
  matrix products  37.6 us (10%)
  local copies, waits for them, and re-layouts  33.7 us (9%)
  starting transfers between devices  21.9 us (6%)
  between operations  14.3 us (4%)
  other arithmetic  13.8 us (4%)
    unnamed x4, waiting for transfers between devices  150 us
    all_gather x2, waiting for transfers between devices, fetch_forward(): return lax.all_gather(shard, 'seq', axis=0, tiled=True)  109 us
    slice x2, local copies, waits for them, and re-layouts, forward_layer(): weight[:, tap, :]  23.7 us
    dot_general x6, matrix products, forward_layer(): jnp.dot(padded[tap * spacing:tap * spacing + length], weight[:, tap, :],...  15.1 us
    dot_general x6, matrix products, backward_layer(): lax.dot_general(grad_pad[start_row:start_row + length], weight[:, tap, :]...  12 us
    ppermute x4, starting transfers between devices, padded_2(): lax.ppermute(lax.slice_in_dim(block, block.shape[dim] - width, None, axis...  12 us
    dot_general x6, matrix products, weight_term(): lax.dot_general(window, grad_out, (((0,), (0,)), ((), ())), preferred_ele...  10.4 us
    ppermute x4, starting transfers between devices, padded_2(): lax.ppermute(lax.slice_in_dim(block, 0, width, axis=dim), axis, backward)  9.84 us
  transfers between devices with their start and end apart: 11, of which 3 were waited for; matrix products, arithmetic and copies ran while one was open for 17% of the time, Pallas kernels for 0%

commit v1 on v0

--- a/solution.py
+++ b/solution.py
@@ -39,7 +39,9 @@
 
 
 def fetch_forward(shard):
-    return lax.all_gather(shard, "seq", axis=0, tiled=True)
+    return jnp.concatenate(
+        lax.all_to_all(jnp.stack(lax.axis_size("seq") * [shard]), "seq", 0, 0), 0
+    )
 
 
 def fetch_backward(shard):

time: 381 us -> 427 us (1.12)
  local copies, waits for them, and re-layouts: 33.7 us -> 57.8 us
  starting transfers between devices: 21.9 us -> 38.9 us
    all_to_all x0 -> x2, waiting for transfers between devices: none -> 45.5 us  [fetch_forward(): lax.all_to_all(jnp.stack(lax.axis_size('seq') * [shard]), 'seq', 0, 0)]
    all_gather x2, waiting for transfers between devices: 109 us -> 65.7 us  [fetch_backward(): return lax.all_gather(shard, 'seq', axis=0, tiled=True)]
    all_to_all x0 -> x2, starting transfers between devices: none -> 18.2 us  [fetch_forward(): lax.all_to_all(jnp.stack(lax.axis_size('seq') * [shard]), 'seq', 0, 0)]
    reshape x0 -> x2, local copies, waits for them, and re-layouts: none -> 13.8 us  [fetch_forward(): jnp.concatenate(lax.all_to_all(jnp.stack(lax.axis_size('seq') * [shard]),...]
    all_to_all x0 -> x2, local copies, waits for them, and re-layouts: none -> 9.71 us  [fetch_forward(): lax.all_to_all(jnp.stack(lax.axis_size('seq') * [shard]), 'seq', 0, 0)]
    another operation x0 -> x2, local copies, waits for them, and re-layouts: none -> 4.99 us  [fetch_forward(): jnp.stack(lax.axis_size('seq') * [shard])]
    unnamed x47 -> x29, local copies, waits for them, and re-layouts: 9.1 us -> 5.05 us
  transfers between devices with their start and end apart: 11 -> 13, of which waited for: 3 -> 4; matrix products, arithmetic and copies ran while one was open for 17% -> 25% of each run, Pallas kernels for 0% -> 0%
where the time goes in v1:
time: 427 us; the launch traced here: 426 us
  waiting for transfers between devices  261 us (61%)
  local copies, waits for them, and re-layouts  57.8 us (14%)
  matrix products  40.6 us (10%)
  starting transfers between devices  38.9 us (9%)
  between operations  14.2 us (3%)
  other arithmetic  13.5 us (3%)
    unnamed x4, waiting for transfers between devices  149 us
    all_gather x2, waiting for transfers between devices, fetch_backward(): return lax.all_gather(shard, 'seq', axis=0, tiled=True)  65.7 us
    all_to_all x2, waiting for transfers between devices, fetch_forward(): lax.all_to_all(jnp.stack(lax.axis_size('seq') * [shard]), 'seq', 0, 0)  45.5 us
    slice x2, local copies, waits for them, and re-layouts, backward_layer(): weight[:, tap, :]  22.5 us
    all_to_all x2, starting transfers between devices, fetch_forward(): lax.all_to_all(jnp.stack(lax.axis_size('seq') * [shard]), 'seq', 0, 0)  18.2 us
    dot_general x6, matrix products, forward_layer(): jnp.dot(padded[tap * spacing:tap * spacing + length], weight[:, tap, :],...  16.9 us
    reshape x2, local copies, waits for them, and re-layouts, fetch_forward(): jnp.concatenate(lax.all_to_all(jnp.stack(lax.axis_size('seq') * [shard]),...  13.8 us
    dot_general x6, matrix products, backward_layer(): lax.dot_general(grad_pad[start_row:start_row + length], weight[:, tap, :]...  13.4 us
  transfers between devices with their start and end apart: 13, of which 4 were waited for; matrix products, arithmetic and copies ran while one was open for 25% of the time, Pallas kernels for 0%

profile of v1, /device:TPU:1, one launch (start us, length us, event | category | flops | bytes accessed | tf_op | source)
XLA Modules:
  0.0 425.6 jit_solution(8928202690675994422)
XLA Ops:
  8.7 2.5 stack.20
  11.2 11.9 %all-to-all-start = ((bf16[128,6,3,768]{3,1,2,0:T(8,128)(2,1)}), bf16[128,6,3,768]{3,1,2,0:T(8,128)(2,1)}, u32[]{:S(2)}, u32[]{:S(2)}) async-start(bf16[128,6,3,768]{3,1,2,0:T(8,128)(2,1)} %stack.20), calls=%async_computation | async-start | bytes 9437184 | tf_op jit(solution)/shard_map/all_to_all | solution.py:43
  24.9 3.0 collective-permute-start.1
  27.9 2.5 collective-permute-start
  31.4 2.4 collective-permute-start.5
  33.8 2.5 collective-permute-start.4
  36.4 45.5 %all-to-all-done = bf16[128,6,3,768]{3,1,2,0:T(8,128)(2,1)} async-done(((bf16[128,6,3,768]{3,1,2,0:T(8,128)(2,1)}), bf16[128,6,3,768]{3,1,2,0:T(8,128)(2,1)}, u32[]{:S(2)}, u32[]{:S(2)}) %all-to-all-start) | async-done | bytes 3538976 | tf_op jit(solution)/shard_map/all_to_all | solution.py:43
  81.9 2.4 stack.21
  84.3 6.3 %all-to-all-start.1 = ((bf16[128,6,3,768]{3,1,2,0:T(8,128)(2,1)}), bf16[128,6,3,768]{3,1,2,0:T(8,128)(2,1)}, u32[]{:S(2)}, u32[]{:S(2)}) async-start(bf16[128,6,3,768]{3,1,2,0:T(8,128)(2,1)} %stack.21), calls=%async_computation.1 | async-start | bytes 9437184 | tf_op jit(solution)/shard_map/all_to_all | solution.py:43
  90.9 4.9 %copy.32 = bf16[128,6,3,768]{3,1,0,2:T(8,128)(2,1)} copy(bf16[128,6,3,768]{3,1,2,0:T(8,128)(2,1)} %all-to-all-done) | data formatting | bytes 7077888 | tf_op jit(solution)/shard_map/all_to_all | solution.py:43
  95.8 6.9 %reshape.42 = bf16[768,3,768]{2,0,1:T(8,128)(2,1)} reshape(bf16[128,6,3,768]{3,1,0,2:T(8,128)(2,1)} %copy.32) | data formatting | bytes 7077888 | tf_op jit(solution)/shard_map/reshape | solution.py:42
  102.7 2.8 fusion.52
  107.8 3.3 fusion.36
  111.1 63.7 %all-gather.3.cloned.1.call-done = bf16[768,3,768]{2,1,0:T(4,128)(2,1)} async-done(((bf16[6,3,768]{2,1,0:T(4,128)(2,1)}), bf16[768,3,768]{2,1,0:T(4,128)(2,1)}) %all-gather.3.cloned.1.call-update) | async-done | bytes 3538960 | tf_op jit(solution)/shard_map/all_gather | solution.py:48
  174.8 11.2 %fusion.69 = (bf16[768,1,768]{2,1,0:T(2,128)(2,1)S(1)}, bf16[768,1,768]{2,1,0:T(2,128)(2,1)S(1)}, bf16[768,1,768]{2,1,0:T(2,128)(2,1)S(1)}) fusion(bf16[768,3,768]{2,1,0:T(4,128)(2,1)} %all-gather.3.cloned.1.call-done), kind=kLoop, calls=%fused_computation.111 | loop fusion | bytes 7077888 | tf_op jit(solution)/shard_map/slice | solution.py:91
  187.5 2.3 fusion.46
  189.9 3.4 fusion.35
  193.3 3.4 fusion.31
  198.6 2.6 collective-permute-start.3
  201.3 2.3 convolution_bitcast_fusion.3
  205.0 2.3 convolution_bitcast_fusion.5
  208.8 3.3 maximum_multiply_fusion
  215.0 3.2 maximum_multiply_fusion.1
  218.2 4.8 %copy.34 = bf16[128,6,3,768]{3,1,0,2:T(8,128)(2,1)} copy(bf16[128,6,3,768]{3,1,2,0:T(8,128)(2,1)} %all-to-all-done.1) | data formatting | bytes 7077888 | tf_op jit(solution)/shard_map/all_to_all | solution.py:43
  223.0 7.0 %reshape.43 = bf16[768,3,768]{2,0,1:T(8,128)(2,1)} reshape(bf16[128,6,3,768]{3,1,0,2:T(8,128)(2,1)} %copy.34) | data formatting | bytes 7077888 | tf_op jit(solution)/shard_map/reshape | solution.py:42
  230.8 3.1 collective-permute-start.7
  236.1 4.3 %fusion.49 = f32[1024,768]{1,0:T(8,128)} fusion(bf16[1024,768]{1,0:T(8,128)(2,1)S(1)} %get-tuple-element.29, bf16[768,3,768]{2,0,1:T(8,128)(2,1)} %reshape.43), kind=kOutput, calls=%fused_computation.75 | convolution fusion | flops 1207959552 | bytes 5898240 | tf_op jit(solution)/shard_map/dot_general | solution.py:57
  242.4 11.2 %fusion.68 = (bf16[768,1,768]{2,1,0:T(2,128)(2,1)S(1)}, bf16[768,1,768]{2,1,0:T(2,128)(2,1)S(1)}, bf16[768,1,768]{2,1,0:T(2,128)(2,1)S(1)}) fusion(bf16[768,3,768]{2,1,0:T(4,128)(2,1)} %all-gather.5.cloned.1.call-done), kind=kLoop, calls=%fused_computation.110 | loop fusion | bytes 7077888 | tf_op jit(solution)/shard_map/slice | solution.py:91
  255.1 2.2 fusion.42
  257.4 2.6 fusion.21
  265.4 2.8 fusion.37
  268.1 148.6 %all-reduce.5.cloned.1.call-done = (f32[768,3,768]{2,0,1:T(8,128)}, f32[768,3,768]{2,0,1:T(8,128)}) async-done(((f32[768,3,768]{2,0,1:T(8,128)}, f32[768,3,768]{2,0,1:T(8,128)}), (f32[768,3,768]{2,0,1:T(8,128)}, f32[768,3,768]{2,0,1:T(8,128)})) %all-reduce.5.cloned.1.call-update) | async-done | bytes 14155792
  (66 shorter events, 29.9 us)
Async XLA Ops:
  7.2 167.7 %all-gather.3.cloned.1.call-start = ((), (), s32[]{:S(2)}) async-start(), calls=%async_computation.2 | async-start | bytes 4755456 | tf_op jit(solution)/shard_map/all_gather | solution.py:48
  11.2 12.0 %copy-start = (bf16[1024,768]{1,0:T(8,128)(2,1)S(1)}, bf16[1024,768]{1,0:T(8,128)(2,1)}, u32[]{:S(2)}) copy-start(bf16[1024,768]{1,0:T(8,128)(2,1)} %param.4) | copy-start | bytes 4718596
  11.2 70.7 %all-to-all-start = ((bf16[128,6,3,768]{3,1,2,0:T(8,128)(2,1)}), bf16[128,6,3,768]{3,1,2,0:T(8,128)(2,1)}, u32[]{:S(2)}, u32[]{:S(2)}) async-start(bf16[128,6,3,768]{3,1,2,0:T(8,128)(2,1)} %stack.20), calls=%async_computation | async-start | bytes 9437184 | tf_op jit(solution)/shard_map/all_to_all | solution.py:43
  23.1 13.3 %copy-start.11 = (bf16[6,3,768]{2,1,0:T(4,128)(2,1)S(1)}, bf16[6,3,768]{2,1,0:T(4,128)(2,1)}, u32[]{:S(2)}) copy-start(bf16[6,3,768]{2,1,0:T(4,128)(2,1)} %param.6) | copy-start | bytes 82948
  23.1 219.3 %all-gather.5.cloned.1.call-start = ((), (), s32[]{:S(2)}) async-start(), calls=%async_computation.3 | async-start | bytes 4755456 | tf_op jit(solution)/shard_map/all_gather | solution.py:48
  24.8 80.7 %copy-start.9 = (bf16[1024,768]{1,0:T(8,128)(2,1)}, bf16[1024,768]{1,0:T(8,128)(2,1)S(1)}, u32[]{:S(2)}) copy-start(bf16[1024,768]{1,0:T(8,128)(2,1)S(1)} %fusion.11) | copy-start | bytes 4718596
  24.9 82.9 %collective-permute-start.1 = (bf16[32,768]{1,0:T(8,128)(2,1)S(1)}, bf16[32,768]{1,0:T(8,128)(2,1)}, u32[]{:S(2)}, u32[]{:S(2)}) collective-permute-start(bf16[32,768]{1,0:T(8,128)(2,1)S(1)} %get-tuple-element.36), channel_id=1, source_target_pairs={{1,0},{2,1},{3,2},{4,3},{5,4},{6,5},{7,6},{8,7},{9,8},{10,9},{11,1... | collective-permute-start | bytes 147464 | tf_op jit(solution)/shard_map/ppermute | solution.py:19
  27.9 77.6 %collective-permute-start = (bf16[32,768]{1,0:T(8,128)(2,1)S(1)}, bf16[32,768]{1,0:T(8,128)(2,1)}, u32[]{:S(2)}, u32[]{:S(2)}) collective-permute-start(bf16[32,768]{1,0:T(8,128)(2,1)S(1)} %get-tuple-element.37), channel_id=1, source_target_pairs={{0,1},{1,2},{2,3},{3,4},{4,5},{5,6},{6,7},{7,8},{8,9},{9,10},{10,1... | collective-permute-start | bytes 147464 | tf_op jit(solution)/shard_map/ppermute | solution.py:16
  31.4 158.4 %collective-permute-start.5 = (bf16[64,768]{1,0:T(8,128)(2,1)S(1)}, bf16[64,768]{1,0:T(8,128)(2,1)}, u32[]{:S(2)}, u32[]{:S(2)}) collective-permute-start(bf16[64,768]{1,0:T(8,128)(2,1)S(1)} %get-tuple-element.32), channel_id=1, source_target_pairs={{0,1},{1,2},{2,3},{3,4},{4,5},{5,6},{6,7},{7,8},{8,9},{9,10},{10,1... | collective-permute-start | bytes 294920 | tf_op jit(solution)/shard_map/ppermute | solution.py:16
  33.8 153.7 %collective-permute-start.4 = (bf16[64,768]{1,0:T(8,128)(2,1)S(1)}, bf16[64,768]{1,0:T(8,128)(2,1)}, u32[]{:S(2)}, u32[]{:S(2)}) collective-permute-start(bf16[64,768]{1,0:T(8,128)(2,1)S(1)} %get-tuple-element.33), channel_id=1, source_target_pairs={{1,0},{2,1},{3,2},{4,3},{5,4},{6,5},{7,6},{8,7},{9,8},{10,9},{11,1... | collective-permute-start | bytes 294920 | tf_op jit(solution)/shard_map/ppermute | solution.py:19
  84.3 133.9 %all-to-all-start.1 = ((bf16[128,6,3,768]{3,1,2,0:T(8,128)(2,1)}), bf16[128,6,3,768]{3,1,2,0:T(8,128)(2,1)}, u32[]{:S(2)}, u32[]{:S(2)}) async-start(bf16[128,6,3,768]{3,1,2,0:T(8,128)(2,1)} %stack.21), calls=%async_computation.1 | async-start | bytes 9437184 | tf_op jit(solution)/shard_map/all_to_all | solution.py:43
  90.7 326.1 %all-reduce.5.cloned.1.call-start = ((), (), s32[]{:S(2)}) async-start(), calls=%async_computation.4 | async-start | bytes 28311552
  102.7 2.9 copy-start.6
  111.1 78.7 %copy-start.4 = (bf16[1024,768]{1,0:T(8,128)(2,1)}, bf16[1024,768]{1,0:T(8,128)(2,1)S(1)}, u32[]{:S(2)}) copy-start(bf16[1024,768]{1,0:T(8,128)(2,1)S(1)} %get-tuple-element.39) | copy-start | bytes 4718596
  174.8 11.2 %copy-start.8 = (bf16[1024,768]{1,0:T(8,128)(2,1)S(1)}, bf16[1024,768]{1,0:T(8,128)(2,1)}, u32[]{:S(2)}) copy-start(bf16[1024,768]{1,0:T(8,128)(2,1)} %param.7) | copy-start | bytes 4718596
  193.2 8.0 %copy-start.10 = (bf16[1024,768]{1,0:T(8,128)(2,1)S(1)}, bf16[1024,768]{1,0:T(8,128)(2,1)}, u32[]{:S(2)}) copy-start(bf16[1024,768]{1,0:T(8,128)(2,1)} %copy-done.9) | copy-start | bytes 4718596
  196.7 8.4 %copy-start.1 = (bf16[1024,768]{1,0:T(8,128)(2,1)}, bf16[1024,768]{1,0:T(8,128)(2,1)S(1)}, u32[]{:S(2)}) copy-start(bf16[1024,768]{1,0:T(8,128)(2,1)S(1)} %get-tuple-element.28) | copy-start | bytes 4718596
  196.7 16.8 %collective-permute-start.2 = (bf16[64,768]{1,0:T(8,128)(2,1)S(1)}, bf16[64,768]{1,0:T(8,128)(2,1)S(1)}, u32[]{:S(2)}, u32[]{:S(2)}) collective-permute-start(bf16[64,768]{1,0:T(8,128)(2,1)S(1)} %get-tuple-element.35), channel_id=1, source_target_pairs={{0,1},{1,2},{2,3},{3,4},{4,5},{5,6},{6,7},{7,8},{8,9},{9,10},{10,1... | collective-permute-start | bytes 294920 | tf_op jit(solution)/shard_map/ppermute | solution.py:16
  198.6 13.4 %collective-permute-start.3 = (bf16[64,768]{1,0:T(8,128)(2,1)S(1)}, bf16[64,768]{1,0:T(8,128)(2,1)S(1)}, u32[]{:S(2)}, u32[]{:S(2)}) collective-permute-start(bf16[64,768]{1,0:T(8,128)(2,1)S(1)} %get-tuple-element.34), channel_id=1, source_target_pairs={{1,0},{2,1},{3,2},{4,3},{5,4},{6,5},{7,6},{8,7},{9,8},{10,9},{11,1... | collective-permute-start | bytes 294920 | tf_op jit(solution)/shard_map/ppermute | solution.py:19
  230.8 26.6 %collective-permute-start.7 = (bf16[32,768]{1,0:T(8,128)(2,1)S(1)}, bf16[32,768]{1,0:T(8,128)(2,1)S(1)}, u32[]{:S(2)}, u32[]{:S(2)}) collective-permute-start(bf16[32,768]{1,0:T(8,128)(2,1)S(1)} %get-tuple-element.30), channel_id=1, source_target_pairs={{0,1},{1,2},{2,3},{3,4},{4,5},{5,6},{6,7},{7,8},{8,9},{9,10},{10,1... | collective-permute-start | bytes 147464 | tf_op jit(solution)/shard_map/ppermute | solution.py:16
  233.9 21.2 %collective-permute-start.6 = (bf16[32,768]{1,0:T(8,128)(2,1)S(1)}, bf16[32,768]{1,0:T(8,128)(2,1)}, u32[]{:S(2)}, u32[]{:S(2)}) collective-permute-start(bf16[32,768]{1,0:T(8,128)(2,1)S(1)} %get-tuple-element.31), channel_id=1, source_target_pairs={{1,0},{2,1},{3,2},{4,3},{5,4},{6,5},{7,6},{8,7},{9,8},{10,9},{11,1... | collective-permute-start | bytes 147464 | tf_op jit(solution)/shard_map/ppermute | solution.py:19
  242.4 11.3 %copy-start.2 = (bf16[1024,768]{1,0:T(8,128)(2,1)S(1)}, bf16[1024,768]{1,0:T(8,128)(2,1)}, u32[]{:S(2)}) copy-start(bf16[1024,768]{1,0:T(8,128)(2,1)} %copy-done.1) | copy-start | bytes 4718596
  260.0 2.7 copy-start.3
  262.8 1.5 copy-start.5
  262.8 2.6 copy-start.7
Sparse Core Ops, SparseCore 0:
  11.0 163.7 all-gather.2
  177.9 64.5 all-gather.4
  247.6 169.1 all-reduce.4
